TPU v7x, 32 devices: a whole 2x2x4 slice. The times are simulated.
32 devices in a mesh: grp: 4 (over z), col: 2 (over y), lay: 4 (over x, core).
Axes of the slice: x: 2, y: 2, z: 4, core: 2. Of those that a mesh axis runs over, the one named last changes fastest.
Arguments:
- salinity: float32 [16, 128, 2048], P('lay', ('grp', 'col')), may hold values from 0.3 to 4.2
- zone_ids: int32 [16, 128, 2048], P('lay', ('grp', 'col')), may hold values from 0 to 7
- flow_speed: float32 [16, 128, 2048], P('lay', ('grp', 'col')), may hold values from 0.5 to 4
- fixed_cells: int32 [16, 128, 2048], P('lay', ('grp', 'col')), may hold values 0 or 1
- dispersivity: float32 [2, 8], replicated, may hold values from 50 to 1000
Outputs:
- salinity_next: float32 [16, 128, 2048], P('lay', 'grp', 'col')
All inputs are finite; a program needn't handle non-finite values. No bound on the sum of `fixed_cells` on one device may be relied on, other than what follows from the above.
Results may differ from a plain program's by a relative error of at most 0.00005.
Values sent between devices are 32-bit elements; how exact they have to be, the bound alone decides.
No kernel may reach another device: no remote copies, remote signals or barrier semaphores. Data moves between devices by JAX's collectives and lax.ppermute only.
A program may use at most 128 MiB of HBM per device.

v0:
```python
import jax
import jax.numpy as jnp
from jax import lax
from jax.sharding import PartitionSpec as P


def shifted(values, stride, line_axis, filler, heading):
    line_axis = line_axis % values.ndim
    length = values.shape[line_axis]
    edge_shape = list(values.shape)
    edge_shape[line_axis] = length
    padding = jnp.full(tuple(edge_shape), filler, values.dtype)
    padded = jnp.concatenate([padding, values, padding], axis=line_axis)
    return lax.dynamic_slice_in_dim(padded, length + heading * stride, length, axis=line_axis)


def reduce_lines(below_coef, middle, above_coef, right_side, line_axis):
    length = middle.shape[line_axis]
    levels = max(1, (length - 1).bit_length())

    def one_level(_, carry):
        below_now, middle_now, above_now, right_now, stride = carry
        weight_below = -below_now / shifted(middle_now, stride, line_axis, 1.0, -1)
        weight_above = -above_now / shifted(middle_now, stride, line_axis, 1.0, 1)
        below_next = weight_below * shifted(below_now, stride, line_axis, 0.0, -1)
        above_next = weight_above * shifted(above_now, stride, line_axis, 0.0, 1)
        middle_next = (
            middle_now
            + weight_below * shifted(above_now, stride, line_axis, 0.0, -1)
            + weight_above * shifted(below_now, stride, line_axis, 0.0, 1)
        )
        right_next = (
            right_now
            + weight_below * shifted(right_now, stride, line_axis, 0.0, -1)
            + weight_above * shifted(right_now, stride, line_axis, 0.0, 1)
        )
        return (below_next, middle_next, above_next, right_next, stride * 2)

    result = lax.fori_loop(
        0, levels, one_level, (below_coef, middle, above_coef, right_side, jnp.int32(1))
    )
    return result[3] / result[1]


def line_solve(coupling, field, line_axis):
    return reduce_lines(-coupling, 1.0 + 2.0 * coupling, -coupling, field, line_axis - field.ndim)


def couplings(zone_ids, flow_speed, fixed_cells, dispersivity):
    opened = 1.0 - fixed_cells.astype(jnp.float32)
    longit = jnp.zeros(flow_speed.shape, jnp.float32)
    transv = jnp.zeros(flow_speed.shape, jnp.float32)
    for number in range(dispersivity.shape[1]):
        matched = zone_ids == number
        longit = jnp.where(matched, dispersivity[0, number], longit)
        transv = jnp.where(matched, dispersivity[1, number], transv)
    return (opened * longit * flow_speed, opened * transv * flow_speed)


def block_parts(field, coupling, line_axis):
    length = field.shape[line_axis]
    places = lax.broadcasted_iota(jnp.int32, field.shape, line_axis)
    firsts = (places == 0).astype(jnp.float32)
    lasts = (places == length - 1).astype(jnp.float32)
    stacked = jnp.stack([field, firsts, lasts])
    solved = reduce_lines(
        -coupling, 1.0 + 2.0 * coupling, -coupling, stacked, line_axis - field.ndim
    )
    interior = solved[0]
    weight_low = lax.index_in_dim(coupling, 0, line_axis, keepdims=True) * solved[1]
    weight_high = lax.index_in_dim(coupling, length - 1, line_axis, keepdims=True) * solved[2]
    edges = jnp.stack(
        [
            lax.index_in_dim(interior, 0, line_axis, keepdims=False),
            lax.index_in_dim(interior, length - 1, line_axis, keepdims=False),
            lax.index_in_dim(weight_low, 0, line_axis, keepdims=False),
            lax.index_in_dim(weight_low, length - 1, line_axis, keepdims=False),
            lax.index_in_dim(weight_high, 0, line_axis, keepdims=False),
            lax.index_in_dim(weight_high, length - 1, line_axis, keepdims=False),
        ]
    )[None]
    return (interior, weight_low, weight_high, edges)


def assemble(interior, weight_low, weight_high, gathered, position, line_axis):
    blocks = gathered.shape[0]
    zeros = jnp.zeros(gathered.shape[2:], jnp.float32)

    def forward(carry, block):
        ratio_prev, last_prev = carry
        first_low = -block[2]
        last_low = -block[3]
        first_high = -block[4]
        last_high = -block[5]
        pivot = 1.0 - first_low * ratio_prev
        factor_first = first_high / pivot
        factor_last = last_high + last_low * ratio_prev * factor_first
        value_first = (block[0] - first_low * last_prev) / pivot
        value_last = last_low * ratio_prev * value_first + block[1] - last_low * last_prev
        return ((factor_last, value_last), (factor_first, factor_last, value_first, value_last))

    _, factors = lax.scan(forward, (zeros, zeros), gathered)

    def backward(first_next, block):
        first_here = block[2] - block[0] * first_next
        last_here = block[3] - block[1] * first_next
        return (first_here, (first_here, last_here))

    _, (firsts, lasts) = lax.scan(backward, zeros, factors, reverse=True)
    last_before = lax.dynamic_index_in_dim(
        lasts, jnp.maximum(position - 1, 0), 0, keepdims=False
    ) * (position > 0).astype(jnp.float32)
    first_after = lax.dynamic_index_in_dim(
        firsts, jnp.minimum(position + 1, blocks - 1), 0, keepdims=False
    ) * (position < blocks - 1).astype(jnp.float32)
    return (
        interior
        + weight_low * jnp.expand_dims(last_before, line_axis)
        + weight_high * jnp.expand_dims(first_after, line_axis)
    )


def per_device(salinity, zone_ids, flow_speed, fixed_cells, dispersivity):
    long_coupling, trans_coupling = couplings(zone_ids, flow_speed, fixed_cells, dispersivity)
    first = line_solve(long_coupling, salinity, 2)
    field = lax.all_to_all(first, "col", split_axis=2, concat_axis=1, tiled=True)
    coupling = lax.all_to_all(trans_coupling, "col", split_axis=2, concat_axis=1, tiled=True)
    interior, weight_low, weight_high, edges = block_parts(field, coupling, 1)
    gathered = lax.all_gather(edges, "grp", axis=0, tiled=True)
    second = assemble(interior, weight_low, weight_high, gathered, lax.axis_index("grp"), 1)
    whole_field, whole_coupling = (
        lax.all_gather(second, "lay", axis=0, tiled=True),
        lax.all_gather(coupling, "lay", axis=0, tiled=True),
    )
    solved = line_solve(whole_coupling, whole_field, 0)
    start = lax.axis_index("lay") * second.shape[0]
    return lax.dynamic_slice_in_dim(solved, start, second.shape[0], 0)


def solution(mesh):
    placed = (
        P("lay", ("grp", "col"), None),
        P("lay", ("grp", "col"), None),
        P("lay", ("grp", "col"), None),
        P("lay", ("grp", "col"), None),
        P(),
    )
    return jax.shard_map(
        per_device, mesh=mesh, in_specs=placed, out_specs=P("lay", "grp", "col"), check_vma=False
    )
```

profile of v0, /device:TPU:0, one launch (start us, length us, event | category | flops | bytes accessed | tf_op | source)
XLA Modules:
  0.0 251.0 jit_solution(15573494215802975976)
XLA Ops:
  6.5 2.0 fusion.24
  8.5 7.0 %multiply_add_fusion.8 = (f32[4,16,2048]{2,1,0:T(8,128)S(1)}, f32[4,16,2048]{2,1,0:T(8,128)S(1)}, pred[4,16,2048]{2,1,0:T(8,128)(4,1)S(1)}, pred[4,16,2048]{2,1,...) fusion(f32[4,16,2048]{2,1,0:T(8,128)} %param.17, ...), kind=kLoop, calls=%fused_computation.76 | loop fusion | flops 2883584 | bytes 3670048 | tf_op jit(solution)/shard_map/add | solution.py:46
  15.6 5.5 %multiply_multiply_fusion.1 = f32[4,16,2048]{2,1,0:T(8,128)S(1)} fusion(f32[4,16,2048]{2,1,0:T(8,128)S(1)} %copy-done.2, pred[4,16,2048]{2,1,0:T(8,128)(4,1)S(1)} %get-tuple-element.469, pred[4,16,2048]{2,1,0:T(8,128)(4,1)S(1)} %get-tuple-element.468, pred[4,16,2048]{2,1,0:T(8,128)(4,1)S(1)} %get-tuple-element.467, ...), kind=kLoop, calls=%fused_computation.79 | loop fusion | flops 1572864 | bytes 2621472 | tf_op jit(solution)/shard_map/mul | solution.py:57
  21.1 3.0 %copy.53 = f32[4,16,2048]{1,0,2:T(4,128)} copy(f32[4,16,2048]{2,1,0:T(8,128)S(1)} %multiply_multiply_fusion.1) | data formatting | bytes 1048576 | tf_op jit(solution)/shard_map/mul | solution.py:57
  24.1 5.5 %reshape.35 = f32[2,1,65536]{2,1,0:T(1,128)} reshape(f32[2048,4,16]{2,1,0:T(4,128)} %bitcast.167) | data formatting | bytes 1048576
  29.6 4.4 %all-to-all-start = ((f32[2,1,65536]{2,1,0:T(1,128)}), f32[2,1,65536]{2,1,0:T(1,128)S(1)}, u32[]{:S(2)}, u32[]{:S(2)}) async-start(f32[2,1,65536]{2,1,0:T(1,128)} %reshape.35), calls=%async_computation | async-start | bytes 1048576 | tf_op jit(solution)/shard_map/all_to_all | solution.py:127
  34.1 22.1 %while.94 = (s32[]{:T(128)}, f32[4,16,2048]{2,1,0:T(8,128)S(1)}, f32[4,16,2048]{2,1,0:T(8,128)S(1)}, f32[4,16,2048]{2,1,0:T(8,128)S(1)}, f32[4,16,2048]{2,1,0:T(...) while((s32[]{:T(128)}, f32[4,16,2048]{2,1,0:T(8,128)S(1)}, ...), condition=%wide.region_1.2_spmd, body=%wide.region_0.1_spmd.sunk | while | flops 4980748 | bytes 18874640 | solution.py:39
  34.9 1.2 dynamic-slice_multiply_fusion.10
  36.9 1.2 dynamic-slice_multiply_fusion.10
  38.9 1.2 dynamic-slice_multiply_fusion.10
  40.9 1.2 dynamic-slice_multiply_fusion.10
  43.0 1.2 dynamic-slice_multiply_fusion.10
  45.0 1.2 dynamic-slice_multiply_fusion.10
  47.0 1.2 dynamic-slice_multiply_fusion.10
  49.0 1.2 dynamic-slice_multiply_fusion.10
  51.0 1.2 dynamic-slice_multiply_fusion.10
  53.1 1.2 dynamic-slice_multiply_fusion.10
  55.1 1.2 dynamic-slice_multiply_fusion.10
  56.4 3.0 %copy.55 = f32[4,16,2048]{1,0,2:T(4,128)} copy(f32[4,16,2048]{2,1,0:T(8,128)S(1)} %div.38) | data formatting | bytes 1048576 | tf_op jit(solution)/shard_map/div | solution.py:42
  59.4 5.5 %reshape.37 = f32[2,1,65536]{2,1,0:T(1,128)} reshape(f32[2048,4,16]{2,1,0:T(4,128)} %bitcast.168) | data formatting | bytes 1048576
  64.9 3.5 %all-to-all-start.1 = ((f32[2,1,65536]{2,1,0:T(1,128)}), f32[2,1,65536]{2,1,0:T(1,128)S(1)}, u32[]{:S(2)}, u32[]{:S(2)}) async-start(f32[2,1,65536]{2,1,0:T(1,128)} %reshape.37), calls=%async_computation.1 | async-start | bytes 1048576 | tf_op jit(solution)/shard_map/all_to_all | solution.py:126
  69.2 2.3 reduce
  71.6 5.0 %reshape.36 = f32[2048,4,16]{2,1,0:T(4,128)} reshape(f32[2,65536]{1,0:T(2,128)S(1)} %reduce) | data formatting | bytes 1048576
  76.6 4.4 %copy.54 = f32[4,2,16,1024]{3,2,1,0:T(8,128)} copy(f32[4,2,16,1024]{2,0,3,1:T(4,128)} %bitcast.169) | data formatting | bytes 1048576 | tf_op jit(solution)/shard_map/all_to_all | solution.py:127
  81.3 1.0 fusion.23
  82.3 1.2 multiply_add_fusion.9
  83.5 2.3 reduce.1
  85.8 5.0 %reshape.38 = f32[2048,4,16]{2,1,0:T(4,128)} reshape(f32[2,65536]{1,0:T(2,128)S(1)} %reduce.1) | data formatting | bytes 1048576
  90.9 4.7 %copy.56 = f32[4,2,16,1024]{3,2,1,0:T(8,128)} copy(f32[4,2,16,1024]{2,0,3,1:T(4,128)} %bitcast.170) | data formatting | bytes 1048576 | tf_op jit(solution)/shard_map/all_to_all | solution.py:126
  95.8 0.8 copy-done.4
  96.8 18.2 %while.95 = (s32[]{:T(128)}, f32[4,32,1024]{2,1,0:T(8,128)S(1)}, f32[4,32,1024]{2,1,0:T(8,128)S(1)}, f32[4,32,1024]{2,1,0:T(8,128)S(1)}, f32[3,4,32,1024]{3,2,1,...) while((s32[]{:T(128)}, f32[4,32,1024]{2,1,0:T(8,128)S(1)}, ...), condition=%wide.region_3.4_spmd, body=%wide.region_2.3_spmd.sunk | while | flops 7602188 | bytes 33554724 | solution.py:39
  99.1 1.2 multiply_add_fusion.13
  102.8 1.2 multiply_add_fusion.13
  106.4 1.2 multiply_add_fusion.13
  110.1 1.2 multiply_add_fusion.13
  113.7 1.2 multiply_add_fusion.13
  115.4 1.1 copy_divide_fusion
  116.9 15.5 %all-gather = f32[24,4,1024]{2,1,0:T(4,128)S(1)} all-gather(f32[6,4,1024]{2,1,0:T(4,128)S(1)} %fusion.14), channel_id=2, replica_groups=mesh['grp'=4,'col'=2,'lay'=4] {'grp'}, dimensions={0}, use_global_device_ids=true | all-gather | bytes 491520 | tf_op jit(solution)/shard_map/all_gather | solution.py:129
  133.4 1.1 copy.59
  134.6 3.6 %multiply_add_fusion.6 = (f32[16,32,1024]{2,1,0:T(8,128)}, f32[16,32,1024]{2,1,0:T(8,128)S(1)}) fusion(f32[16,32,1024]{2,1,0:T(8,128)} %all-gather.4.cloned.1.call-done), kind=kLoop, calls=%fused_computation.66 | loop fusion | flops 1572864 | bytes 6291456 | tf_op jit(solution)/shard_map/add | solution.py:46
  138.2 1.3 copy.148
  139.5 20.0 %all-gather.6.cloned.1.call-done = f32[16,32,1024]{2,1,0:T(8,128)} async-done(((f32[4,32,1024]{2,1,0:T(8,128)}), f32[16,32,1024]{2,1,0:T(8,128)}) %all-gather.6.cloned.1.call-update) | async-done | bytes 2097168 | tf_op jit(solution)/shard_map/all_gather | solution.py:132
  159.5 82.6 %while.96 = (s32[]{:T(128)}, f32[16,32,1024]{2,1,0:T(8,128)S(1)}, f32[16,32,1024]{2,1,0:T(8,128)}, f32[16,32,1024]{2,1,0:T(8,128)}, f32[16,32,1024]{2,1,0:T(8,12...) while((s32[]{:T(128)}, f32[16,32,1024]{2,1,0:T(8,128)S(1)}, ...), condition=%wide.region_9.10_spmd, body=%wide.region_8.9_spmd.sunk | while | flops 19922956 | bytes 83886376 | solution.py:39
  159.7 1.3 copy-done
  161.1 0.9 pad_maximum_fusion.30
  162.0 1.6 broadcast.160
  163.6 7.9 %pad_maximum_fusion.29 = (f32[48,32,1024]{2,1,0:T(8,128)S(1)}, f32[48,32,1024]{2,1,0:T(8,128)}, f32[48,32,1024]{2,1,0:T(8,128)}) fusion(f32[16,32,1024]{2,1,0:T(8,128)} %broadcast.160, f32[16,32,1024]{2,1,0:T(8,128)} %get-tuple-element.970, f32[16,32,1024]{2,1,0:T(8,128)} %get-tuple-element.969, f32[16,32,1024]{2,1,0:T(8,128)S(1)} %get-tuple-element.967), kind=kLoop, calls=%fused_computation.25.clone.1 | loop fusion | flops 9437184 | bytes 27262976 | tf_op jit(solution)/shard_map/while/body/eval_jaxpr/concatenate | solution.py:13
  171.5 8.5 %dynamic-slice_multiply_fusion.13 = (f32[16,32,1024]{2,1,0:T(8,128)}, f32[16,32,1024]{2,1,0:T(8,128)}, f32[16,32,1024]{2,1,0:T(8,128)S(1)}, f32[16,32,1024]{2,1,0:T(8,128)}) fusion(f32[48,32,1024]{2,1,0:T(8,128)} %get-tuple-element.758, s32[]{:T(128)S(6)} %select_n.145, f32[48,32,1024]{2,1,0:T(8,128)S(1)} %pad_maximum_fusion.30, ...), kind=kLoop, calls=%fused_computation.33.clone.1 | loop fusion | flops 7340032 | bytes 33554440 | tf_op jit(solution)/shard_map/while/body/eval_jaxpr/mul | solution.py:26
  180.2 1.3 copy-done
  181.6 0.9 pad_maximum_fusion.30
  182.5 1.6 broadcast.160
  184.1 7.9 %pad_maximum_fusion.29 = (f32[48,32,1024]{2,1,0:T(8,128)S(1)}, f32[48,32,1024]{2,1,0:T(8,128)}, f32[48,32,1024]{2,1,0:T(8,128)}) fusion(f32[16,32,1024]{2,1,0:T(8,128)} %broadcast.160, f32[16,32,1024]{2,1,0:T(8,128)} %get-tuple-element.970, f32[16,32,1024]{2,1,0:T(8,128)} %get-tuple-element.969, f32[16,32,1024]{2,1,0:T(8,128)S(1)} %get-tuple-element.967), kind=kLoop, calls=%fused_computation.25.clone.1 | loop fusion | flops 9437184 | bytes 27262976 | tf_op jit(solution)/shard_map/while/body/eval_jaxpr/concatenate | solution.py:13
  192.0 8.5 %dynamic-slice_multiply_fusion.13 = (f32[16,32,1024]{2,1,0:T(8,128)}, f32[16,32,1024]{2,1,0:T(8,128)}, f32[16,32,1024]{2,1,0:T(8,128)S(1)}, f32[16,32,1024]{2,1,0:T(8,128)}) fusion(f32[48,32,1024]{2,1,0:T(8,128)} %get-tuple-element.758, s32[]{:T(128)S(6)} %select_n.145, f32[48,32,1024]{2,1,0:T(8,128)S(1)} %pad_maximum_fusion.30, ...), kind=kLoop, calls=%fused_computation.33.clone.1 | loop fusion | flops 7340032 | bytes 33554440 | tf_op jit(solution)/shard_map/while/body/eval_jaxpr/mul | solution.py:26
  200.8 1.3 copy-done
  202.1 0.9 pad_maximum_fusion.30
  203.0 1.6 broadcast.160
  204.6 7.9 %pad_maximum_fusion.29 = (f32[48,32,1024]{2,1,0:T(8,128)S(1)}, f32[48,32,1024]{2,1,0:T(8,128)}, f32[48,32,1024]{2,1,0:T(8,128)}) fusion(f32[16,32,1024]{2,1,0:T(8,128)} %broadcast.160, f32[16,32,1024]{2,1,0:T(8,128)} %get-tuple-element.970, f32[16,32,1024]{2,1,0:T(8,128)} %get-tuple-element.969, f32[16,32,1024]{2,1,0:T(8,128)S(1)} %get-tuple-element.967), kind=kLoop, calls=%fused_computation.25.clone.1 | loop fusion | flops 9437184 | bytes 27262976 | tf_op jit(solution)/shard_map/while/body/eval_jaxpr/concatenate | solution.py:13
  212.5 9.0 %dynamic-slice_multiply_fusion.13 = (f32[16,32,1024]{2,1,0:T(8,128)}, f32[16,32,1024]{2,1,0:T(8,128)}, f32[16,32,1024]{2,1,0:T(8,128)S(1)}, f32[16,32,1024]{2,1,0:T(8,128)}) fusion(f32[48,32,1024]{2,1,0:T(8,128)} %get-tuple-element.758, s32[]{:T(128)S(6)} %select_n.145, f32[48,32,1024]{2,1,0:T(8,128)S(1)} %pad_maximum_fusion.30, ...), kind=kLoop, calls=%fused_computation.33.clone.1 | loop fusion | flops 7340032 | bytes 33554440 | tf_op jit(solution)/shard_map/while/body/eval_jaxpr/mul | solution.py:26
  221.8 1.3 copy-done
  223.1 0.9 pad_maximum_fusion.30
  224.1 1.6 broadcast.160
  225.6 7.9 %pad_maximum_fusion.29 = (f32[48,32,1024]{2,1,0:T(8,128)S(1)}, f32[48,32,1024]{2,1,0:T(8,128)}, f32[48,32,1024]{2,1,0:T(8,128)}) fusion(f32[16,32,1024]{2,1,0:T(8,128)} %broadcast.160, f32[16,32,1024]{2,1,0:T(8,128)} %get-tuple-element.970, f32[16,32,1024]{2,1,0:T(8,128)} %get-tuple-element.969, f32[16,32,1024]{2,1,0:T(8,128)S(1)} %get-tuple-element.967), kind=kLoop, calls=%fused_computation.25.clone.1 | loop fusion | flops 9437184 | bytes 27262976 | tf_op jit(solution)/shard_map/while/body/eval_jaxpr/concatenate | solution.py:13
  233.6 8.5 %dynamic-slice_multiply_fusion.13 = (f32[16,32,1024]{2,1,0:T(8,128)}, f32[16,32,1024]{2,1,0:T(8,128)}, f32[16,32,1024]{2,1,0:T(8,128)S(1)}, f32[16,32,1024]{2,1,0:T(8,128)}) fusion(f32[48,32,1024]{2,1,0:T(8,128)} %get-tuple-element.758, s32[]{:T(128)S(6)} %select_n.145, f32[48,32,1024]{2,1,0:T(8,128)S(1)} %pad_maximum_fusion.30, ...), kind=kLoop, calls=%fused_computation.33.clone.1 | loop fusion | flops 7340032 | bytes 33554440 | tf_op jit(solution)/shard_map/while/body/eval_jaxpr/mul | solution.py:26
  242.1 2.1 dynamic-slice_divide_fusion.6
  (137 shorter events, 25.0 us)
Async XLA Ops:
  6.5 9.0 %copy-start.2 = (f32[4,16,2048]{2,1,0:T(8,128)S(1)}, f32[4,16,2048]{2,1,0:T(8,128)}, u32[]{:S(2)}) copy-start(f32[4,16,2048]{2,1,0:T(8,128)} %param.17) | copy-start | bytes 1572868
  6.5 9.0 %copy-start.3 = (s32[4,16,2048]{2,1,0:T(8,128)S(1)}, s32[4,16,2048]{2,1,0:T(8,128)}, u32[]{:S(2)}) copy-start(s32[4,16,2048]{2,1,0:T(8,128)} %param.18) | copy-start | bytes 1572868
  29.6 4.5 %copy-start.1 = (f32[4,16,2048]{2,1,0:T(8,128)S(1)}, f32[4,16,2048]{2,1,0:T(8,128)}, u32[]{:S(2)}) copy-start(f32[4,16,2048]{2,1,0:T(8,128)} %param.15) | copy-start | bytes 1572868
  29.6 35.3 %all-to-all-start = ((f32[2,1,65536]{2,1,0:T(1,128)}), f32[2,1,65536]{2,1,0:T(1,128)S(1)}, u32[]{:S(2)}, u32[]{:S(2)}) async-start(f32[2,1,65536]{2,1,0:T(1,128)} %reshape.35), calls=%async_computation | async-start | bytes 1048576 | tf_op jit(solution)/shard_map/all_to_all | solution.py:127
  64.9 18.6 %all-to-all-start.1 = ((f32[2,1,65536]{2,1,0:T(1,128)}), f32[2,1,65536]{2,1,0:T(1,128)S(1)}, u32[]{:S(2)}, u32[]{:S(2)}) async-start(f32[2,1,65536]{2,1,0:T(1,128)} %reshape.37), calls=%async_computation.1 | async-start | bytes 1048576 | tf_op jit(solution)/shard_map/all_to_all | solution.py:126
  68.4 66.1 %all-gather.4.cloned.1.call-start = ((), (), s32[]{:S(2)}) async-start(), calls=%async_computation.2 | async-start | bytes 2621440 | tf_op jit(solution)/shard_map/all_gather | solution.py:133
  81.1 78.4 %all-gather.6.cloned.1.call-start = ((), (), s32[]{:S(2)}) async-start(), calls=%async_computation.3 | async-start | bytes 2621440 | tf_op jit(solution)/shard_map/all_gather | solution.py:132
  95.6 1.1 copy-start.4
  159.5 1.6 copy-start
  180.0 1.6 copy-start
  200.5 1.6 copy-start
  221.5 1.6 copy-start
Sparse Core Ops, SparseCore 0:
  81.2 24.9 all-gather.3
  134.7 24.7 all-gather.5
where the time goes:
time: 252 us; the launch traced here: 251 us
  other arithmetic  133 us (53%)
  local copies, waits for them, and re-layouts  58.6 us (23%)
  waiting for transfers between devices  20 us (8%)
  blocking collectives  15.5 us (6%)
  between operations  13.8 us (5%)
  starting transfers between devices  8.38 us (3%)
    mul x20, other arithmetic, one_level(): above_next = weight_above * shifted(above_now, stride, line_axis, 0.0, 1)  49.3 us
    concatenate x29, other arithmetic, shifted(): padded = jnp.concatenate([padding, values, padding], axis=line_axis)  48.9 us
    unnamed x21, local copies, waits for them, and re-layouts  23.3 us
    all_gather x1, waiting for transfers between devices, per_device(): lax.all_gather(second, 'lay', axis=0, tiled=True)  20 us
    all_gather x1, blocking collectives, per_device(): gathered = lax.all_gather(edges, 'grp', axis=0, tiled=True)  15.5 us
    add x2, other arithmetic, line_solve(): 1.0 + 2.0 * coupling  10.6 us
    another operation x51, local copies, waits for them, and re-layouts  9.4 us
    add x5, other arithmetic, one_level(): right_now + weight_below * shifted(right_now, stride, line_axis, 0.0, -1)  6.12 us
  transfers between devices with their start and end apart: 4, of which 1 were waited for; matrix products, arithmetic and copies ran while one was open for 33% of the time, Pallas kernels for 0%

commit v1 on v0

v1 whole, which is shorter than its diff:
```python
import functools

import jax
import jax.numpy as jnp
from jax import lax
from jax.experimental import pallas as pl
from jax.experimental.pallas import tpu as pltpu
from jax.sharding import PartitionSpec as P

LANES = 128
SUB = 8
F32 = jnp.float32
VMEM = pl.BlockSpec(memory_space=pltpu.VMEM)
SMEM = pl.BlockSpec(memory_space=pltpu.SMEM)
GRANT = 24 << 20


def call(body, outs, n_in, name, scratch=(), smem=(), flops=1 << 20, moved=1 << 21):
    return pl.pallas_call(
        body,
        out_shape=outs,
        in_specs=[SMEM if i in smem else VMEM for i in range(n_in)],
        out_specs=[VMEM] * len(outs),
        scratch_shapes=list(scratch),
        compiler_params=pltpu.CompilerParams(vmem_limit_bytes=GRANT),
        cost_estimate=pl.CostEstimate(flops=flops, bytes_accessed=moved, transcendentals=0),
        name=name,
    )


def shape(*dims):
    return jax.ShapeDtypeStruct(dims, F32)


def lookup(bits, values):
    level = list(values)
    for bit in bits:
        level = [jnp.where(bit, high, low) for low, high in zip(level[::2], level[1::2])]
    return level[0]


def coupling_body(n_col, tiles, zones, zone, flow, fixed, disp, longc, *parts):
    mine = lax.axis_index("col")
    depth = max(1, (zones - 1).bit_length())
    row = lambda which: [disp[which, min(i, zones - 1)] for i in range(1 << depth)]
    along, across = row(0), row(1)
    for k in range(n_col):
        first_tile = lax.rem(mine + k, n_col) * tiles
        for t in range(tiles):
            j = first_tile + t
            ids = zone[:, :, j]
            bits = [(ids & (1 << b)) != 0 for b in range(depth)]
            opened = 1.0 - fixed[:, :, j].astype(F32)
            speed = flow[:, :, j]
            longc[j] = opened * lookup(bits, along) * speed
            parts[k][t] = opened * lookup(bits, across) * speed


def shift_up(x, stride, wrap, sub, lines):
    lead = x.shape[0]
    if stride < SUB:
        later = jnp.concatenate([x[1:], pltpu.roll(x[:1], wrap, 2)], axis=0)
        return pltpu.roll(jnp.where(sub < stride, later, x), SUB - stride, 1)
    blocks = stride // SUB
    if blocks < lead:
        return jnp.concatenate([x[blocks:], pltpu.roll(x[:blocks], wrap, 2)], axis=0)
    return pltpu.roll(x, LANES - lines * (blocks // lead), 2)


def shift_down(x, stride, wrap, sub, lines):
    lead = x.shape[0]
    if stride < SUB:
        earlier = jnp.concatenate([pltpu.roll(x[-1:], LANES - wrap, 2), x[:-1]], axis=0)
        return pltpu.roll(jnp.where(sub >= SUB - stride, earlier, x), stride, 1)
    blocks = stride // SUB
    if blocks < lead:
        return jnp.concatenate([pltpu.roll(x[-blocks:], LANES - wrap, 2), x[:-blocks]], axis=0)
    return pltpu.roll(x, lines * (blocks // lead), 2)


def column_body(n_col, tiles, sal, longc, *rest):
    outs, (tc, td, g_s, l_s, d_s, xs) = rest[:n_col], rest[n_col:]
    n_j = longc.shape[0]
    lines = longc.shape[1] * longc.shape[2] * SUB
    halves = LANES // lines
    blocks = n_j // halves
    step = LANES // SUB
    for b in range(blocks):
        block = jnp.concatenate(
            [longc[h * blocks + b].reshape(lines, LANES) for h in range(halves)], axis=0
        )
        tc[b] = block.T
        block = jnp.concatenate(
            [sal[:, :, h * blocks + b].reshape(lines, LANES) for h in range(halves)], axis=0
        )
        td[b] = block.T

    full = (blocks, SUB, LANES)
    sub = lax.broadcasted_iota(jnp.int32, full, 1)
    lane = lax.broadcasted_iota(jnp.int32, full, 2)
    lead = lax.broadcasted_iota(jnp.int32, full, 0)
    begins = (sub == 0) & (lead == 0) & (lane < lines)
    ends = (sub == SUB - 1) & (lead == blocks - 1) & (lane >= LANES - lines)

    at = lambda ref, q: ref[:, pl.ds(q, SUB, stride=step), :]
    g = low = d = None
    for q in range(step - 1):
        s = at(tc, q)
        r = at(td, q)
        if q == 0:
            inv = 1.0 / (1.0 + 2.0 * s)
            g = s * inv
            low = jnp.where(begins, 0.0, g)
            d = r * inv
        else:
            inv = 1.0 / ((1.0 + 2.0 * s) - s * g)
            g = s * inv
            low = g * low
            d = r * inv + g * d
        g_s[q] = g
        l_s[q] = low
        d_s[q] = d
    f_d, f_l, f_u = d, low, g
    for q in range(step - 3, -1, -1) if step > 2 else ():
        gq = g_s[q]
        f_d = d_s[q] + gq * f_d
        f_l = l_s[q] + gq * f_l
        f_u = gq * f_u
    up = functools.partial(shift_up, wrap=LANES - lines, sub=sub, lines=lines)
    down = functools.partial(shift_down, wrap=LANES - lines, sub=sub, lines=lines)
    n_d = jnp.where(ends, 0.0, up(f_d, 1))
    n_l = jnp.where(ends, 0.0, up(f_l, 1))
    n_u = jnp.where(ends, 0.0, up(f_u, 1))
    s = at(tc, step - 1)
    r = at(td, step - 1)
    inv = 1.0 / ((1.0 + 2.0 * s) - s * g - s * n_l)
    si = s * inv
    a = si * low
    c = si * n_u
    x = r * inv + si * (d + n_d)
    stride = 1
    total = n_j * SUB
    while stride < total:
        a_d, a_u = down(a, stride), up(a, stride)
        c_d, c_u = down(c, stride), up(c, stride)
        x_d, x_u = down(x, stride), up(x, stride)
        inv = 1.0 / (1.0 - a * c_d - c * a_u)
        x = (x + a * x_d + c * x_u) * inv
        a = a * a_d * inv
        c = c * c_u * inv
        stride *= 2
    before = down(x, 1)
    td[:, pl.ds(step - 1, SUB, stride=step), :] = x
    for q in range(step - 2, -1, -1):
        x = d_s[q] + l_s[q] * before + g_s[q] * x
        td[:, pl.ds(q, SUB, stride=step), :] = x
    for b in range(blocks):
        block = td[b].T
        for h in range(halves):
            xs[h * blocks + b] = block[h * lines : (h + 1) * lines].reshape(xs.shape[1:])
    mine = lax.axis_index("col")
    for k in range(n_col):
        outs[k][...] = xs[pl.ds(lax.rem(mine + k, n_col) * tiles, tiles)]


def row_tile(ref, layer, row):
    return ref[:, layer * row[1] + row[0], :]


def rows_in_order(parts, held, n_col):
    mine = lax.axis_index("col")
    for k, part in enumerate(parts):
        held[lax.rem(mine + n_col - k, n_col)] = part[...].reshape(held.shape[1:])


def row_factor_body(n_col, layers, rows, *refs):
    parts = refs[:n_col]
    t_out, h_out, g_out, l_out, u_out, edges, held = refs[n_col:]
    tiles = held.shape[1] // (layers * rows)
    rows_in_order(parts, held, n_col)

    def load(source, row):
        return jnp.stack(
            [
                held[source, pl.ds(layer * rows + row, tiles, stride=layers * rows), :]
                for layer in range(layers)
            ]
        )

    def forward(source, carry):
        g, low = carry
        for row in range(rows):
            s = load(source, row)
            inv = 1.0 / ((1.0 + 2.0 * s) - s * g)
            g = s * inv
            low = g * low
            at = source * rows + row
            t_out[at] = s
            h_out[at] = inv
            g_out[at] = g
            l_out[at] = low
        return g, low

    zero = jnp.zeros((layers, tiles, LANES), F32)
    g, low = lax.fori_loop(0, n_col, forward, (zero, zero + 1.0), unroll=n_col <= 2)
    total = n_col * rows
    u_out[total - 1] = g
    edges[2] = low
    edges[3] = g

    def backward(turn, carry):
        low, high = carry
        source = n_col - 1 - turn
        for row in range(rows - 1, -1, -1):
            at = source * rows + row
            gq = g_out[at]
            low = l_out[at] + gq * low
            high = gq * high
            l_out[at] = low
            u_out[at] = high
        return low, high

    low, high = lax.fori_loop(0, n_col, backward, (zero, zero + 1.0), unroll=n_col <= 2)
    edges[0] = low
    edges[1] = high


def row_sweep_body(n_col, layers, rows, *refs):
    parts = refs[:n_col]
    h, g, d_out, edges, held = refs[n_col:]
    tiles = held.shape[1] // (layers * rows)
    rows_in_order(parts, held, n_col)

    def forward(source, d):
        for row in range(rows):
            r = jnp.stack(
                [
                    held[source, pl.ds(layer * rows + row, tiles, stride=layers * rows), :]
                    for layer in range(layers)
                ]
            )
            at = source * rows + row
            d = r * h[at] + g[at] * d
            d_out[at] = d
        return d

    zero = jnp.zeros((layers, tiles, LANES), F32)
    d = lax.fori_loop(0, n_col, forward, zero, unroll=n_col <= 2)
    edges[1] = d

    def backward(turn, d):
        source = n_col - 1 - turn
        for row in range(rows - 1, -1, -1):
            at = source * rows + row
            d = d_out[at] + g[at] * d
            d_out[at] = d
        return d

    d = lax.fori_loop(0, n_col, backward, zero, unroll=n_col <= 2)
    edges[0] = d


def row_join_body(n_grp, *refs):
    coefs, fields = refs[:n_grp], refs[n_grp : 2 * n_grp]
    d_in, l_in, u_in, out, co, fi, firsts, lasts = refs[2 * n_grp :]
    mine = lax.axis_index("grp")
    for k in range(n_grp):
        block = lax.rem(mine + n_grp - k, n_grp)
        co[block] = coefs[k][...]
        fi[block] = fields[k][...]
    zero = jnp.zeros(fi.shape[2:], F32)
    p, q = zero, zero
    steps = []
    for b in range(n_grp):
        f_l, f_u, l_l, l_u = (co[b, i] for i in range(4))
        inv = 1.0 / (1.0 - f_l * q)
        start = (fi[b, 0] + f_l * p) * inv
        ratio = f_u * inv
        link = l_l * q
        p = fi[b, 1] + l_l * p + link * start
        q = l_u + link * ratio
        steps.append((start, ratio, p, q))
    after = zero
    firsts[n_grp] = zero
    lasts[0] = zero
    for b in range(n_grp - 1, -1, -1):
        start, ratio, p, q = steps[b]
        lasts[b + 1] = p + q * after
        after = start + ratio * after
        firsts[b] = after
    before, after = lasts[mine], firsts[mine + 1]

    total, unit = d_in.shape[0], 8

    def one(i, _):
        at = pl.ds(i * unit, unit)
        out[at] = d_in[at] + l_in[at] * before + u_in[at] * after
        return 0

    lax.fori_loop(0, total // unit, one, 0, unroll=total // unit <= 4)


def layer_order(m, half, layers, total):
    along = jnp.where(half == 0, m, total - 1 - m)
    return along // layers, lax.rem(along, layers)


def own_and_half(n_lay):
    mine = lax.axis_index("lay")
    n_half = max(n_lay // 2, 1)
    return lax.rem(mine, n_half), mine // n_half, n_half


def gather_half(parts, held, n_lay):
    place, half, n_half = own_and_half(n_lay)
    for k, part in enumerate(parts):
        held[lax.rem(place + n_half - k, n_half)] = part[...]
    return place, half, n_half


UNIT = 8


def layer_factor_body(n_lay, *refs):
    n_half = max(n_lay // 2, 1)
    parts = refs[:n_half]
    h_out, g_out, last, held = refs[n_half:]
    place, half, n_half = gather_half(parts, held, n_lay)
    layers, rows = held.shape[2], held.shape[1]
    total = n_half * layers

    def one(i, _):
        at = pl.ds(i * UNIT, UNIT)
        g = None
        for m in range(total):
            device, layer = layer_order(m, half, layers, total)
            s = held[device, at, layer]
            pivot = 1.0 + 2.0 * s
            if m:
                pivot = pivot - s * g
            inv = 1.0 / pivot
            g = s * inv
            h_out[m, at] = inv
            g_out[m, at] = g
        last[at] = g
        return 0

    lax.fori_loop(0, rows // UNIT, one, 0)


def layer_sweep_body(n_lay, *refs):
    n_half = max(n_lay // 2, 1)
    parts = refs[:n_half]
    h, g, d_out, last, held = refs[n_half:]
    place, half, n_half = gather_half(parts, held, n_lay)
    layers, rows = held.shape[2], held.shape[1]
    total = n_half * layers

    def one(i, _):
        at = pl.ds(i * UNIT, UNIT)
        d = None
        for m in range(total):
            device, layer = layer_order(m, half, layers, total)
            r = held[device, at, layer] * h[m, at]
            d = r if m == 0 else r + g[m, at] * d
            d_out[m, at] = d
        last[at] = d
        return 0

    lax.fori_loop(0, rows // UNIT, one, 0)


def layer_join_body(n_lay, other_d, other_g, d_in, g_in, out, solved):
    place, half, n_half = own_and_half(n_lay)
    total, rows, tiles = d_in.shape[0], d_in.shape[1], d_in.shape[2]
    layers = total // n_half
    groups = rows // SUB

    def one(i, _):
        at = pl.ds(i * UNIT, UNIT)
        g = g_in[total - 1, at]
        x = (d_in[total - 1, at] + g * other_d[at]) / (1.0 - g * other_g[at])
        solved[total - 1] = x
        for m in range(total - 2, -1, -1):
            x = d_in[m, at] + g_in[m, at] * x
            solved[m] = x
        for layer in range(layers):
            along = place * layers + layer
            m = jnp.where(half == 0, along, total - 1 - along)
            values = solved[m]
            for r in range(SUB):
                start = (layer * groups + i) * tiles * SUB + r
                out[pl.ds(start, tiles, stride=SUB), :] = values[r]
        return 0

    lax.fori_loop(0, groups, one, 0)


def solution(mesh):
    n_grp, n_col, n_lay = (mesh.shape[a] for a in ("grp", "col", "lay"))
    n_half = max(n_lay // 2, 1)

    def hop(value, axis, size, k):
        return lax.ppermute(value, axis, [(i, (i + k) % size) for i in range(size)])

    def hop_half(value, k):
        pairs = [
            (h * n_half + i, h * n_half + (i + k) % n_half)
            for h in range(n_lay // n_half)
            for i in range(n_half)
        ]
        return lax.ppermute(value, "lay", pairs)

    def across(value):
        return lax.ppermute(value, "lay", [(i, n_lay - 1 - i) for i in range(n_lay)])

    def per_device(salinity, zone_ids, flow_speed, fixed_cells, dispersivity):
        layers, rows, length = salinity.shape
        n_j = length // LANES
        tiles = n_j // n_col
        groups = rows // SUB
        total = rows * n_col

        def tiled(x):
            return x.reshape(layers, groups, SUB, n_j, LANES).transpose(0, 1, 3, 2, 4)

        part = shape(tiles, layers, groups, SUB, LANES)
        whole = shape(n_j, layers, groups, SUB, LANES)
        zones = dispersivity.shape[1]
        longc, *t_parts = call(
            functools.partial(coupling_body, n_col, tiles, zones),
            [whole] + [part] * n_col,
            4,
            "couplings",
            smem=(3,),
        )(tiled(zone_ids), tiled(flow_speed), tiled(fixed_cells), dispersivity)
        t_parts = [t_parts[0]] + [hop(t_parts[k], "col", n_col, k) for k in range(1, n_col)]

        lines = layers * rows
        blocks = n_j * lines // LANES
        step = LANES // SUB
        square = pltpu.VMEM((blocks, LANES, LANES), F32)
        chain = pltpu.VMEM((step - 1, blocks, SUB, LANES), F32)
        parts = call(
            functools.partial(column_body, n_col, tiles),
            [part] * n_col,
            2,
            "columns",
            [square, square, chain, chain, chain, pltpu.VMEM(whole.shape, F32)],
        )(tiled(salinity), longc)
        parts = [parts[0]] + [hop(parts[k], "col", n_col, k) for k in range(1, n_col)]

        line = (layers, tiles, LANES)
        held = pltpu.VMEM((n_col, tiles * layers * rows, LANES), F32)
        field = shape(total, *line)
        t, h, g, low, high, coefs = call(
            functools.partial(row_factor_body, n_col, layers, rows),
            [field] * 5 + [shape(4, *line)],
            n_col,
            "row_factor",
            [held],
        )(*t_parts)
        coefs = [coefs] + [hop(coefs, "grp", n_grp, k) for k in range(1, n_grp)]
        t_half = [t] + [hop_half(t, k) for k in range(1, n_half)]
        stacked = shape(n_half * layers, total, tiles, LANES)
        plane = shape(total, tiles, LANES)
        held_half = pltpu.VMEM((n_half, total, *line), F32)
        lh, lg, ratio = call(
            functools.partial(layer_factor_body, n_lay),
            [stacked, stacked, plane],
            n_half,
            "layer_factor",
            [held_half],
        )(*t_half)
        other_ratio = across(ratio)

        d, edges = call(
            functools.partial(row_sweep_body, n_col, layers, rows),
            [field, shape(2, *line)],
            n_col + 2,
            "row_sweep",
            [held],
        )(*parts, h, g)
        edges = [edges] + [hop(edges, "grp", n_grp, k) for k in range(1, n_grp)]
        (second,) = call(
            functools.partial(row_join_body, n_grp),
            [field],
            2 * n_grp + 3,
            "row_join",
            [
                pltpu.VMEM((n_grp, 4, *line), F32),
                pltpu.VMEM((n_grp, 2, *line), F32),
                pltpu.VMEM((n_grp + 1, *line), F32),
                pltpu.VMEM((n_grp + 1, *line), F32),
            ],
        )(*coefs, *edges, d, low, high)

        halves = [second] + [hop_half(second, k) for k in range(1, n_half)]
        ld, last = call(
            functools.partial(layer_sweep_body, n_lay),
            [stacked, plane],
            n_half + 2,
            "layer_sweep",
            [held_half],
        )(*halves, lh, lg)
        (out,) = call(
            functools.partial(layer_join_body, n_lay),
            [shape(layers * total * tiles, LANES)],
            4,
            "layer_join",
            [pltpu.VMEM((n_half * layers, UNIT, tiles, LANES), F32)],
        )(across(last), other_ratio, ld, lg)
        out = out.reshape(layers, total // SUB, tiles, SUB, LANES).transpose(0, 1, 3, 2, 4)
        return out.reshape(layers, total, tiles * LANES)

    placed = (P("lay", ("grp", "col"), None),) * 4 + (P(),)
    return jax.shard_map(
        per_device, mesh=mesh, in_specs=placed, out_specs=P("lay", "grp", "col"), check_vma=False
    )
```

time: 252 us -> 44.9 us (0.18)
  other arithmetic: 133 us -> 0 us
  local copies, waits for them, and re-layouts: 58.6 us -> 3.81 us
  blocking collectives: 15.5 us -> 0 us
  between operations: 13.8 us -> 0.07 us
  starting transfers between devices: 8.38 us -> 14.8 us
  Pallas kernels: 0 us -> 5.6 us
    mul x29 -> x0, other arithmetic: 55.5 us -> none  [the longest x20 49.3 us: one_level(): above_next = weight_above * shifted(above_now, stride, line_axis, 0.0, 1)]
    concatenate x29 -> x0, other arithmetic: 48.9 us -> none  [shifted(): padded = jnp.concatenate([padding, values, padding], axis=line_axis)]
    add x14 -> x0, other arithmetic: 20.6 us -> none  [the longest x2 10.6 us: line_solve(): 1.0 + 2.0 * coupling]
    ppermute x0 -> x12, waiting for transfers between devices: none -> 20.4 us  [the longest x8 15.4 us: hop(): return lax.ppermute(value, axis, [(i, (i + k) % size) for i in range(size)])]
    all_gather x2 -> x0, waiting for transfers between devices: 20 us -> none  [the longest x1 20 us: per_device(): lax.all_gather(second, 'lay', axis=0, tiled=True)]
    unnamed x21 -> x10, local copies, waits for them, and re-layouts: 23.3 us -> 3.81 us
    all_gather x1 -> x0, blocking collectives: 15.5 us -> none  [per_device(): gathered = lax.all_gather(edges, 'grp', axis=0, tiled=True)]
    ppermute x0 -> x12, starting transfers between devices: none -> 14.8 us  [the longest x8 12 us: hop(): return lax.ppermute(value, axis, [(i, (i + k) % size) for i in range(size)])]
  transfers between devices with their start and end apart: 4 -> 12, of which waited for: 1 -> 6; matrix products, arithmetic and copies ran while one was open for 33% -> 0% of each run, Pallas kernels for 0% -> 7%
where the time goes in v1:
time: 44.9 us; the launch traced here: 44.6 us
  waiting for transfers between devices  20.4 us (45%)
  starting transfers between devices  14.8 us (33%)
  Pallas kernels  5.6 us (12%)
  local copies, waits for them, and re-layouts  3.81 us (8%)
    ppermute x8, waiting for transfers between devices, hop(): return lax.ppermute(value, axis, [(i, (i + k) % size) for i in range(size)])  15.4 us
    ppermute x8, starting transfers between devices, hop(): return lax.ppermute(value, axis, [(i, (i + k) % size) for i in range(size)])  12 us
    ppermute x2, waiting for transfers between devices, across(): lax.ppermute(value, 'lay', [(i, n_lay - 1 - i) for i in range(n_lay)])  4.92 us
    unnamed x10, local copies, waits for them, and re-layouts  3.81 us
    ppermute x2, starting transfers between devices, across(): lax.ppermute(value, 'lay', [(i, n_lay - 1 - i) for i in range(n_lay)])  2.76 us
    pallas_call x1, Pallas kernels, per_device(): call(functools.partial(column_body, n_col, tiles), [part] * n_col, 2, 'co...  1.6 us
    pallas_call x1, Pallas kernels, per_device(): call(functools.partial(coupling_body, n_col, tiles, zones), [whole] + [pa...  1.1 us
    pallas_call x1, Pallas kernels, per_device(): call(functools.partial(layer_join_body, n_lay), [shape(layers * total * t...  1.01 us
  transfers between devices with their start and end apart: 12, of which 6 were waited for; matrix products, arithmetic and copies ran while one was open for 0% of the time, Pallas kernels for 7%

profile of v1, /device:TPU:0, one launch (start us, length us, event | category | flops | bytes accessed | tf_op | source)
XLA Modules:
  0.0 44.6 jit_solution(3556237636732459670)
XLA Ops:
  0.0 0.0 copy-start.4
  0.0 0.7 %copy-done.4 = f32[2,8]{1,0:T(2,128)S(1)} copy-done((f32[2,8]{1,0:T(2,128)S(1)}, f32[2,8]{1,0:T(2,128)}, u32[]{:S(2)}) %copy-start.4) | copy-done | bytes 88
  0.7 0.0 copy-start.1
  0.7 1.0 %copy-done.1 = s32[4,16,2048]{2,1,0:T(8,128)S(1)} copy-done((s32[4,16,2048]{2,1,0:T(8,128)S(1)}, s32[4,16,2048]{2,1,0:T(8,128)}, u32[]{:S(2)}) %copy-start.1) | copy-done | bytes 524312
  1.7 0.0 copy-start.2
  1.7 1.0 %copy-done.2 = f32[4,16,2048]{2,1,0:T(8,128)S(1)} copy-done((f32[4,16,2048]{2,1,0:T(8,128)S(1)}, f32[4,16,2048]{2,1,0:T(8,128)}, u32[]{:S(2)}) %copy-start.2) | copy-done | bytes 524312
  2.8 0.0 copy-start.3
  2.8 1.0 %copy-done.3 = s32[4,16,2048]{2,1,0:T(8,128)S(1)} copy-done((s32[4,16,2048]{2,1,0:T(8,128)S(1)}, s32[4,16,2048]{2,1,0:T(8,128)}, u32[]{:S(2)}) %copy-start.3) | copy-done | bytes 524312
  3.8 0.0 copy-start
  3.8 1.1 %couplings.1 = (f32[16,4,2,8,128]{4,3,2,1,0:T(8,128)S(1)}, f32[8,4,2,8,128]{4,3,2,1,0:T(8,128)S(1)}, f32[8,4,2,8,128]{4,3,2,1,0:T(8,128)S(1)}) custom-call(s32[4,2,16,8,128]{4,3,2,1,0:T(8,128)S(1)} %bitcast.18, f32[4,2,16,8,128]{4,3,2,1,0:T(8,128)S(1)} %bitcast.19, s32[4,2,16,8,128]{4,3,2,1,0:T(8,128)S(1)} %bitcast.20, f32[2,8]{1,0:T(2,128)S(1)} %copy-done.4), custom_call_target="tpu_custom_call" | custom-call | flops 1048576 | bytes 2097152 | tf_op jit(solution)/shard_map/couplings/pallas_call | solution.py:430
  4.9 3.1 %collective-permute-start = (f32[8,4,2,8,128]{4,3,2,1,0:T(8,128)S(1)}, f32[8,4,2,8,128]{4,3,2,1,0:T(8,128)S(1)}, u32[]{:S(2)}, u32[]{:S(2)}) collective-permute-start(f32[8,4,2,8,128]{4,3,2,1,0:T(8,128)S(1)} %get-tuple-element.24), channel_id=1, source_target_pairs={{0,4},{4,0},{1,5},{5,1},{2,6},{6,2},{3,7},{7,3},{8,12},{12,8},{9,1... | collective-permute-start | bytes 786440 | tf_op jit(solution)/shard_map/ppermute | solution.py:404
  8.0 0.0 copy-done
  8.0 1.6 %columns.1 = (f32[8,4,2,8,128]{4,3,2,1,0:T(8,128)S(1)}, f32[8,4,2,8,128]{4,3,2,1,0:T(8,128)S(1)}) custom-call(f32[4,2,16,8,128]{4,3,2,1,0:T(8,128)S(1)} %bitcast.17, f32[16,4,2,8,128]{4,3,2,1,0:T(8,128)S(1)} %get-tuple-element.26.longc), custom_call_target="tpu_custom_call" | custom-call | flops 1048576 | bytes 2097152 | tf_op jit(solution)/shard_map/columns/pallas_call | solution.py:444
  9.6 0.1 collective-permute-start.4
  9.7 5.5 %collective-permute-done.refs_1_ = f32[8,4,2,8,128]{4,3,2,1,0:T(8,128)S(1)} collective-permute-done((f32[8,4,2,8,128]{4,3,2,1,0:T(8,128)S(1)}, f32[8,4,2,8,128]{4,3,2,1,0:T(8,128)S(1)}, u32[]{:S(2)}, u32[]{:S(2)}) %collective-permute-start) | collective-permute-done | bytes 262176 | tf_op jit(solution)/shard_map/ppermute | solution.py:404
  15.1 0.5 %row_factor.1 = (f32[32,4,8,128]{3,2,1,0:T(8,128)S(1)}, f32[32,4,8,128]{3,2,1,0:T(8,128)S(1)}, f32[32,4,8,128]{3,2,1,0:T(8,128)S(1)}, f32[32,4,8,128]{3,2,1,0:T(...) custom-call(f32[8,4,2,8,128]{4,3,2,1,0:T(8,128)S(1)} %get-tuple-element.23.refs_0_, ...), custom_call_target="tpu_custom_call" | custom-call | flops 1048576 | bytes 2097152 | tf_op jit(solution)/shard_map/row_factor/pallas_call | solution.py:456
  15.6 4.3 %collective-permute-done.4.refs_1_ = f32[8,4,2,8,128]{4,3,2,1,0:T(8,128)S(1)} collective-permute-done((f32[8,4,2,8,128]{4,3,2,1,0:T(8,128)S(1)}, f32[8,4,2,8,128]{4,3,2,1,0:T(8,128)S(1)}, u32[]{:S(2)}, u32[]{:S(2)}) %collective-permute-start.4) | collective-permute-done | bytes 262176 | tf_op jit(solution)/shard_map/ppermute | solution.py:404
  19.9 0.4 row_sweep.1
  20.3 3.9 %collective-permute-start.7 = (f32[2,4,8,128]{3,2,1,0:T(8,128)S(1)}, f32[2,4,8,128]{3,2,1,0:T(8,128)S(1)}, u32[]{:S(2)}, u32[]{:S(2)}) collective-permute-start(f32[2,4,8,128]{3,2,1,0:T(8,128)S(1)} %get-tuple-element.31.refs_4_), channel_id=1, source_target_pairs={{0,24},{8,0},{16,8},{24,16},{1,25},{9,1},{17,9},{25,17},{2,26},{10... | collective-permute-start | bytes 98312 | tf_op jit(solution)/shard_map/ppermute | solution.py:404
  24.2 0.4 %collective-permute-start.3 = (f32[4,4,8,128]{3,2,1,0:T(8,128)S(1)}, f32[4,4,8,128]{3,2,1,0:T(8,128)S(1)}, u32[]{:S(2)}, u32[]{:S(2)}) collective-permute-start(f32[4,4,8,128]{3,2,1,0:T(8,128)S(1)} %get-tuple-element.25.refs_0_), channel_id=1, source_target_pairs={{0,24},{8,0},{16,8},{24,16},{1,25},{9,1},{17,9},{25,17},{2,26},{10... | collective-permute-start | bytes 196616 | tf_op jit(solution)/shard_map/ppermute | solution.py:404
  24.7 0.0 collective-permute-start.2
  24.7 1.6 %collective-permute-start.1 = (f32[4,4,8,128]{3,2,1,0:T(8,128)S(1)}, f32[4,4,8,128]{3,2,1,0:T(8,128)S(1)}, u32[]{:S(2)}, u32[]{:S(2)}) collective-permute-start(f32[4,4,8,128]{3,2,1,0:T(8,128)S(1)} %get-tuple-element.25.refs_0_), channel_id=1, source_target_pairs={{0,8},{8,16},{16,24},{24,0},{1,9},{9,17},{17,25},{25,1},{2,10},{10... | collective-permute-start | bytes 196616 | tf_op jit(solution)/shard_map/ppermute | solution.py:404
  26.2 2.9 %collective-permute-start.6 = (f32[2,4,8,128]{3,2,1,0:T(8,128)S(1)}, f32[2,4,8,128]{3,2,1,0:T(8,128)S(1)}, u32[]{:S(2)}, u32[]{:S(2)}) collective-permute-start(f32[2,4,8,128]{3,2,1,0:T(8,128)S(1)} %get-tuple-element.31.refs_4_), channel_id=1, source_target_pairs={{0,16},{8,24},{16,0},{24,8},{1,17},{9,25},{17,1},{25,9},{2,18},{10... | collective-permute-start | bytes 98312 | tf_op jit(solution)/shard_map/ppermute | solution.py:404
  29.2 0.0 collective-permute-done.7.refs_7_
  29.2 0.0 collective-permute-start.5
  29.2 3.7 %collective-permute-done.6.refs_6_ = f32[2,4,8,128]{3,2,1,0:T(8,128)S(1)} collective-permute-done((f32[2,4,8,128]{3,2,1,0:T(8,128)S(1)}, f32[2,4,8,128]{3,2,1,0:T(8,128)S(1)}, u32[]{:S(2)}, u32[]{:S(2)}) %collective-permute-start.6) | collective-permute-done | bytes 32800 | tf_op jit(solution)/shard_map/ppermute | solution.py:404
  32.9 0.0 collective-permute-start.9
  32.9 2.0 %collective-permute-done.5.refs_5_ = f32[2,4,8,128]{3,2,1,0:T(8,128)S(1)} collective-permute-done((f32[2,4,8,128]{3,2,1,0:T(8,128)S(1)}, f32[2,4,8,128]{3,2,1,0:T(8,128)S(1)}, u32[]{:S(2)}, u32[]{:S(2)}) %collective-permute-start.5) | collective-permute-done | bytes 32800 | tf_op jit(solution)/shard_map/ppermute | solution.py:404
  34.9 0.0 collective-permute-done.3.refs_3_
  34.9 0.0 collective-permute-done.2.refs_2_
  34.9 0.0 collective-permute-done.1.refs_1_
  34.9 0.2 row_join.1.refs_0_
  35.1 0.1 collective-permute-start.8
  35.2 0.0 collective-permute-done.9.refs_1_
  35.2 0.4 layer_factor.1
  35.6 1.6 %collective-permute-start.11 = (f32[32,8,128]{2,1,0:T(8,128)S(1)}, f32[32,8,128]{2,1,0:T(8,128)S(1)}, u32[]{:S(2)}, u32[]{:S(2)}) collective-permute-start(f32[32,8,128]{2,1,0:T(8,128)S(1)} %get-tuple-element.39), channel_id=1, source_target_pairs={{0,3},{1,2},{2,1},{3,0},{4,7},{5,6},{6,5},{7,4},{8,11},{9,10},{10,... | collective-permute-start | bytes 393224 | tf_op jit(solution)/shard_map/ppermute | solution.py:415
  37.3 0.0 collective-permute-done.8.refs_1_
  37.3 0.3 layer_sweep.1
  37.6 1.1 %collective-permute-start.10 = (f32[32,8,128]{2,1,0:T(8,128)S(1)}, f32[32,8,128]{2,1,0:T(8,128)S(1)}, u32[]{:S(2)}, u32[]{:S(2)}) collective-permute-start(f32[32,8,128]{2,1,0:T(8,128)S(1)} %get-tuple-element.38), channel_id=1, source_target_pairs={{0,3},{1,2},{2,1},{3,0},{4,7},{5,6},{6,5},{7,4},{8,11},{9,10},{10,... | collective-permute-start | bytes 393224 | tf_op jit(solution)/shard_map/ppermute | solution.py:415
  38.7 2.4 %collective-permute-done.11.other_g = f32[32,8,128]{2,1,0:T(8,128)S(1)} collective-permute-done((f32[32,8,128]{2,1,0:T(8,128)S(1)}, f32[32,8,128]{2,1,0:T(8,128)S(1)}, u32[]{:S(2)}, u32[]{:S(2)}) %collective-permute-start.11) | collective-permute-done | bytes 131104 | tf_op jit(solution)/shard_map/ppermute | solution.py:415
  41.2 2.5 %collective-permute-done.10.other_d = f32[32,8,128]{2,1,0:T(8,128)S(1)} collective-permute-done((f32[32,8,128]{2,1,0:T(8,128)S(1)}, f32[32,8,128]{2,1,0:T(8,128)S(1)}, u32[]{:S(2)}, u32[]{:S(2)}) %collective-permute-start.10) | collective-permute-done | bytes 131104 | tf_op jit(solution)/shard_map/ppermute | solution.py:415
  43.6 1.0 %layer_join.1 = f32[1024,128]{1,0:T(8,128)} custom-call(f32[32,8,128]{2,1,0:T(8,128)S(1)} %collective-permute-done.10.other_d, f32[32,8,128]{2,1,0:T(8,128)S(1)} %collective-permute-done.11.other_g, f32[8,32,8,128]{3,2,1,0:T(8,128)S(1)} %get-tuple-element.40.d_in, f32[8,32,8,128]{3,2,1,0:T(8,128)S(1)} %get-tuple-element.37.refs_3_.g_in), custom_call_target="tpu_custom_call" | custom-call | flops 1048576 | bytes 2097152 | tf_op jit(solution)/shard_map/layer_join/pallas_call | solution.py:506
Async XLA Ops:
  0.0 0.7 %copy-start.4 = (f32[2,8]{1,0:T(2,128)S(1)}, f32[2,8]{1,0:T(2,128)}, u32[]{:S(2)}) copy-start(f32[2,8]{1,0:T(2,128)} %disp.1) | copy-start | bytes 196
  0.7 1.0 %copy-start.1 = (s32[4,16,2048]{2,1,0:T(8,128)S(1)}, s32[4,16,2048]{2,1,0:T(8,128)}, u32[]{:S(2)}) copy-start(s32[4,16,2048]{2,1,0:T(8,128)} %param.6) | copy-start | bytes 1572868
  1.7 1.0 %copy-start.2 = (f32[4,16,2048]{2,1,0:T(8,128)S(1)}, f32[4,16,2048]{2,1,0:T(8,128)}, u32[]{:S(2)}) copy-start(f32[4,16,2048]{2,1,0:T(8,128)} %param.7) | copy-start | bytes 1572868
  2.8 1.0 %copy-start.3 = (s32[4,16,2048]{2,1,0:T(8,128)S(1)}, s32[4,16,2048]{2,1,0:T(8,128)}, u32[]{:S(2)}) copy-start(s32[4,16,2048]{2,1,0:T(8,128)} %param.8) | copy-start | bytes 1572868
  3.8 4.2 %copy-start = (f32[4,16,2048]{2,1,0:T(8,128)S(1)}, f32[4,16,2048]{2,1,0:T(8,128)}, u32[]{:S(2)}) copy-start(f32[4,16,2048]{2,1,0:T(8,128)} %param.5) | copy-start | bytes 1572868
  4.9 10.2 %collective-permute-start = (f32[8,4,2,8,128]{4,3,2,1,0:T(8,128)S(1)}, f32[8,4,2,8,128]{4,3,2,1,0:T(8,128)S(1)}, u32[]{:S(2)}, u32[]{:S(2)}) collective-permute-start(f32[8,4,2,8,128]{4,3,2,1,0:T(8,128)S(1)} %get-tuple-element.24), channel_id=1, source_target_pairs={{0,4},{4,0},{1,5},{5,1},{2,6},{6,2},{3,7},{7,3},{8,12},{12,8},{9,1... | collective-permute-start | bytes 786440 | tf_op jit(solution)/shard_map/ppermute | solution.py:404
  9.6 10.3 %collective-permute-start.4 = (f32[8,4,2,8,128]{4,3,2,1,0:T(8,128)S(1)}, f32[8,4,2,8,128]{4,3,2,1,0:T(8,128)S(1)}, u32[]{:S(2)}, u32[]{:S(2)}) collective-permute-start(f32[8,4,2,8,128]{4,3,2,1,0:T(8,128)S(1)} %get-tuple-element.28), channel_id=1, source_target_pairs={{0,4},{4,0},{1,5},{5,1},{2,6},{6,2},{3,7},{7,3},{8,12},{12,8},{9,1... | collective-permute-start | bytes 786440 | tf_op jit(solution)/shard_map/ppermute | solution.py:404
  20.3 8.8 %collective-permute-start.7 = (f32[2,4,8,128]{3,2,1,0:T(8,128)S(1)}, f32[2,4,8,128]{3,2,1,0:T(8,128)S(1)}, u32[]{:S(2)}, u32[]{:S(2)}) collective-permute-start(f32[2,4,8,128]{3,2,1,0:T(8,128)S(1)} %get-tuple-element.31.refs_4_), channel_id=1, source_target_pairs={{0,24},{8,0},{16,8},{24,16},{1,25},{9,1},{17,9},{25,17},{2,26},{10... | collective-permute-start | bytes 98312 | tf_op jit(solution)/shard_map/ppermute | solution.py:404
  24.2 10.7 %collective-permute-start.3 = (f32[4,4,8,128]{3,2,1,0:T(8,128)S(1)}, f32[4,4,8,128]{3,2,1,0:T(8,128)S(1)}, u32[]{:S(2)}, u32[]{:S(2)}) collective-permute-start(f32[4,4,8,128]{3,2,1,0:T(8,128)S(1)} %get-tuple-element.25.refs_0_), channel_id=1, source_target_pairs={{0,24},{8,0},{16,8},{24,16},{1,25},{9,1},{17,9},{25,17},{2,26},{10... | collective-permute-start | bytes 196616 | tf_op jit(solution)/shard_map/ppermute | solution.py:404
  24.7 10.2 %collective-permute-start.2 = (f32[4,4,8,128]{3,2,1,0:T(8,128)S(1)}, f32[4,4,8,128]{3,2,1,0:T(8,128)S(1)}, u32[]{:S(2)}, u32[]{:S(2)}) collective-permute-start(f32[4,4,8,128]{3,2,1,0:T(8,128)S(1)} %get-tuple-element.25.refs_0_), channel_id=1, source_target_pairs={{0,16},{8,24},{16,0},{24,8},{1,17},{9,25},{17,1},{25,9},{2,18},{10... | collective-permute-start | bytes 196616 | tf_op jit(solution)/shard_map/ppermute | solution.py:404
  24.7 10.2 %collective-permute-start.1 = (f32[4,4,8,128]{3,2,1,0:T(8,128)S(1)}, f32[4,4,8,128]{3,2,1,0:T(8,128)S(1)}, u32[]{:S(2)}, u32[]{:S(2)}) collective-permute-start(f32[4,4,8,128]{3,2,1,0:T(8,128)S(1)} %get-tuple-element.25.refs_0_), channel_id=1, source_target_pairs={{0,8},{8,16},{16,24},{24,0},{1,9},{9,17},{17,25},{25,1},{2,10},{10... | collective-permute-start | bytes 196616 | tf_op jit(solution)/shard_map/ppermute | solution.py:404
  26.2 6.6 %collective-permute-start.6 = (f32[2,4,8,128]{3,2,1,0:T(8,128)S(1)}, f32[2,4,8,128]{3,2,1,0:T(8,128)S(1)}, u32[]{:S(2)}, u32[]{:S(2)}) collective-permute-start(f32[2,4,8,128]{3,2,1,0:T(8,128)S(1)} %get-tuple-element.31.refs_4_), channel_id=1, source_target_pairs={{0,16},{8,24},{16,0},{24,8},{1,17},{9,25},{17,1},{25,9},{2,18},{10... | collective-permute-start | bytes 98312 | tf_op jit(solution)/shard_map/ppermute | solution.py:404
  29.2 5.7 %collective-permute-start.5 = (f32[2,4,8,128]{3,2,1,0:T(8,128)S(1)}, f32[2,4,8,128]{3,2,1,0:T(8,128)S(1)}, u32[]{:S(2)}, u32[]{:S(2)}) collective-permute-start(f32[2,4,8,128]{3,2,1,0:T(8,128)S(1)} %get-tuple-element.31.refs_4_), channel_id=1, source_target_pairs={{0,8},{8,16},{16,24},{24,0},{1,9},{9,17},{17,25},{25,1},{2,10},{10... | collective-permute-start | bytes 98312 | tf_op jit(solution)/shard_map/ppermute | solution.py:404
  32.9 2.3 %collective-permute-start.9 = (f32[32,4,8,128]{3,2,1,0:T(8,128)S(1)}, f32[32,4,8,128]{3,2,1,0:T(8,128)S(1)}, u32[]{:S(2)}, u32[]{:S(2)}) collective-permute-start(f32[32,4,8,128]{3,2,1,0:T(8,128)S(1)} %get-tuple-element.35.refs_0_), channel_id=1, source_target_pairs={{0,1},{1,0},{2,3},{3,2},{4,5},{5,4},{6,7},{7,6},{8,9},{9,8},{10,11... | collective-permute-start | bytes 1572872 | tf_op jit(solution)/shard_map/ppermute | solution.py:412
  35.1 2.2 %collective-permute-start.8 = (f32[32,4,8,128]{3,2,1,0:T(8,128)S(1)}, f32[32,4,8,128]{3,2,1,0:T(8,128)S(1)}, u32[]{:S(2)}, u32[]{:S(2)}) collective-permute-start(f32[32,4,8,128]{3,2,1,0:T(8,128)S(1)} %row_join.1.refs_0_), channel_id=1, source_target_pairs={{0,1},{1,0},{2,3},{3,2},{4,5},{5,4},{6,7},{7,6},{8,9},{9,8},{10,11... | collective-permute-start | bytes 1572872 | tf_op jit(solution)/shard_map/ppermute | solution.py:412
  35.6 5.5 %collective-permute-start.11 = (f32[32,8,128]{2,1,0:T(8,128)S(1)}, f32[32,8,128]{2,1,0:T(8,128)S(1)}, u32[]{:S(2)}, u32[]{:S(2)}) collective-permute-start(f32[32,8,128]{2,1,0:T(8,128)S(1)} %get-tuple-element.39), channel_id=1, source_target_pairs={{0,3},{1,2},{2,1},{3,0},{4,7},{5,6},{6,5},{7,4},{8,11},{9,10},{10,... | collective-permute-start | bytes 393224 | tf_op jit(solution)/shard_map/ppermute | solution.py:415
  37.6 6.0 %collective-permute-start.10 = (f32[32,8,128]{2,1,0:T(8,128)S(1)}, f32[32,8,128]{2,1,0:T(8,128)S(1)}, u32[]{:S(2)}, u32[]{:S(2)}) collective-permute-start(f32[32,8,128]{2,1,0:T(8,128)S(1)} %get-tuple-element.38), channel_id=1, source_target_pairs={{0,3},{1,2},{2,1},{3,0},{4,7},{5,6},{6,5},{7,4},{8,11},{9,10},{10,... | collective-permute-start | bytes 393224 | tf_op jit(solution)/shard_map/ppermute | solution.py:415
